TPU v7x, 256 devices: a whole 4x4x8 slice. The times are simulated.
256 devices in a mesh: lat: 4 (over x_lo, core), lon: 64 (over x_hi, y, z).
Axes of the slice: x: 4 (x_hi: 2, x_lo: 2; x = x_hi * 2 + x_lo), y: 4, z: 8, core: 2. Of those that a mesh axis runs over, the one named last changes fastest.
Arguments:
- field: bfloat16 [512, 2048, 128], P('lat', 'lon'), may hold values from -6 to 6
- land: int32 [512, 2048], P('lat', 'lon'), may hold values 0 or 1
- mirror: int32 [2048], replicated, may hold values from 0 to 2047, as said below
- depth_weight: bfloat16 [49, 128], replicated, may hold values from -2 to 2
- norm_gain: bfloat16 [128], replicated, may hold values from 0.5 to 2
- up_weight: bfloat16 [128, 512], replicated, may hold values from -0.5 to 0.5
- up_bias: bfloat16 [512], replicated, may hold values from -3 to 3
- down_proj: bfloat16 [512, 128], replicated, may hold values from -0.25 to 0.25
- layer_scale: bfloat16 [128], replicated, may hold values from 0.25 to 1
- section_gain: bfloat16 [3, 128], replicated, may hold values from 0.5 to 2
- section_weight: bfloat16 [3, 512, 128], replicated, may hold values from -0.25 to 0.25
- section_bias: bfloat16 [3, 128], replicated, may hold values from -3 to 3
- cotangent: bfloat16 [64, 256, 128], P('lat', 'lon'), may hold values from -6 to 6
Outputs:
- bottleneck: bfloat16 [64, 256, 128], P('lat', 'lon')
- grad_field: bfloat16 [512, 2048, 128], P('lat', 'lon')
- grad_depth: float32 [49, 128], replicated
- grad_up: float32 [128, 512], replicated
- grad_down: float32 [512, 128], replicated
- grad_section: float32 [3, 512, 128], replicated
Inputs may be any that keep to these rules, and one draw needn't show every extreme that they name: mirror[i] = (s - i) mod 2048 for one s, the same for all i; mirror is its own inverse.
All inputs are finite; a program needn't handle non-finite values. No bound on the sum of `land` on one device may be relied on, other than what follows from the above.
Results may differ from a plain program's by a relative error of at most 0.017.
Values may be sent and summed in bfloat16 or wider, within the bound.
A program may use at most 128 MiB of HBM per device.

v0:
```python
import math
import jax
import jax.numpy as jnp
from jax import lax
from jax.sharding import PartitionSpec as P

SECTIONS = 3
epsilon = 1e-06


def extended_2(array, sides, width, wrap):
    for axis, dim in sides:
        peers, length = (lax.axis_size(axis), array.shape[dim])
        up = [(i, (i + 1) % peers) for i in range(peers if wrap else peers - 1)]
        down = [(j, i) for i, j in up]
        last = lax.slice_in_dim(array, length - width, length, axis=dim)
        leading = lax.slice_in_dim(array, 0, width, axis=dim)
        before = lax.ppermute(last, axis, up)
        after = lax.ppermute(leading, axis, down)
        array = jnp.concatenate([before, array, after], axis=dim)
    return array


def norm_parts(values):
    center = values - jnp.mean(values, axis=-1, keepdims=True)
    rstd = lax.rsqrt(jnp.mean(center * center, axis=-1, keepdims=True) + epsilon)
    return (center * rstd, rstd)


def norm_back(grad_hat, normed_hat, rstd):
    first = jnp.mean(grad_hat, axis=-1, keepdims=True)
    second = jnp.mean(grad_hat * normed_hat, axis=-1, keepdims=True)
    return rstd * (grad_hat - first - normed_hat * second)


def gelu_parts(hidden):
    cdf = 0.5 * (1.0 + jax.scipy.special.erf(hidden * 0.7071067811865476))
    dens = jnp.exp(-0.5 * hidden * hidden) * 0.3989422804014327
    return (hidden * cdf, cdf + hidden * dens)


def extend(values):
    widened = extended_2(values, (("lon", 1),), 3, True)
    return extended_2(widened, (("lat", 0),), 3, False)


def on_device(
    field,
    land,
    mirror,
    depth_weight,
    norm_gain,
    up_weight,
    up_bias,
    down_proj,
    layer_scale,
    section_gain,
    section_weight,
    section_bias,
    cotangent,
):
    row_count, col_count, chan_count = field.shape
    lon_count = lax.axis_size("lon")
    total_cols = col_count * lon_count
    total_rows = row_count * lax.axis_size("lat")
    lon_place = lax.axis_index("lon")
    north = lax.axis_index("lat") == lax.axis_size("lat") - 1
    factor = 1.0 / math.sqrt(total_rows * total_cols / 64.0)
    taps = depth_weight.astype(jnp.float32)
    extended = extend(field)
    top_rows = field[row_count - 3 :][::-1]
    every_top = lax.all_gather(top_rows, "lon", axis=1, tiled=True)
    ext_index = jnp.mod(
        lon_place * col_count - 3 + jnp.arange(col_count + 6, dtype=jnp.int32), total_cols
    )
    folded = jnp.take(every_top, jnp.take(mirror, ext_index), axis=1)
    extended = jnp.concatenate(
        [extended[: row_count + 3], jnp.where(north, folded, extended[row_count + 3 :])], axis=0
    )
    depth_out = jnp.zeros((row_count, col_count, chan_count), jnp.float32)
    for tap in range(49):
        tap_row = tap // 7
        tap_col = tap % 7
        depth_out = (
            depth_out
            + extended[tap_row : tap_row + row_count, tap_col : tap_col + col_count].astype(
                jnp.float32
            )
            * taps[tap]
        )
    depth_hat, depth_rstd = norm_parts(depth_out)
    normed = (depth_hat * norm_gain.astype(jnp.float32)).astype(jnp.bfloat16)
    flat = normed.reshape(-1, chan_count)
    hidden = jnp.dot(flat, up_weight, preferred_element_type=jnp.float32) + up_bias.astype(
        jnp.float32
    )
    active_full, slope = gelu_parts(hidden)
    active = active_full.astype(jnp.bfloat16)
    mixed = jnp.dot(active, down_proj, preferred_element_type=jnp.float32).reshape(
        row_count, col_count, chan_count
    )
    land_f = land.astype(jnp.float32)[:, :, None]
    scale_f = layer_scale.astype(jnp.float32)
    level = (land_f * (field.astype(jnp.float32) + scale_f * mixed)).astype(jnp.bfloat16)
    saved = []
    for section in range(SECTIONS):
        section_hat, section_rstd = norm_parts(level.astype(jnp.float32))
        section_norm = (section_hat * section_gain[section].astype(jnp.float32)).astype(
            jnp.bfloat16
        )
        size_r = section_norm.shape[0]
        size_c = section_norm.shape[1]
        patches = section_norm.reshape(size_r // 2, 2, size_c // 2, 2, chan_count)
        kernel = section_weight[section].reshape(2, 2, chan_count, chan_count)
        level = (
            jnp.einsum("iajbc,abcd->ijd", patches, kernel, preferred_element_type=jnp.float32)
            + section_bias[section].astype(jnp.float32)
        ).astype(jnp.bfloat16)
        saved.append((section_hat, section_rstd, patches, kernel))
    upstream = cotangent
    section_list = [None] * SECTIONS
    for section in range(SECTIONS - 1, -1, -1):
        section_hat, section_rstd, patches, kernel = saved[section]
        section_list[section] = jnp.einsum(
            "iajbc,ijd->abcd", patches, upstream, preferred_element_type=jnp.float32
        ).reshape(4 * chan_count, chan_count)
        spread = jnp.einsum(
            "ijd,abcd->iajbc", upstream, kernel, preferred_element_type=jnp.float32
        ).reshape(section_hat.shape)
        upstream = norm_back(
            spread * section_gain[section].astype(jnp.float32), section_hat, section_rstd
        ).astype(jnp.bfloat16)
    section_total = jnp.stack(section_list)
    direct = land_f * upstream.astype(jnp.float32)
    mix_grad = (direct * scale_f).astype(jnp.bfloat16).reshape(-1, chan_count)
    down_sums = jnp.dot(active.T, mix_grad, preferred_element_type=jnp.float32)
    act_grad = jnp.dot(mix_grad, down_proj.T, preferred_element_type=jnp.float32)
    hidden_grad = (act_grad * slope).astype(jnp.bfloat16)
    up_sums = jnp.dot(flat.T, hidden_grad, preferred_element_type=jnp.float32)
    normed_grad = jnp.dot(hidden_grad, up_weight.T, preferred_element_type=jnp.float32).reshape(
        row_count, col_count, chan_count
    )
    depth_grad = norm_back(
        normed_grad * norm_gain.astype(jnp.float32), depth_hat, depth_rstd
    ).astype(jnp.bfloat16)
    depth_f = depth_grad.astype(jnp.float32)
    tap_list = []
    for tap in range(49):
        tap_row = tap // 7
        tap_col = tap % 7
        tap_list.append(
            jnp.sum(
                extended[tap_row : tap_row + row_count, tap_col : tap_col + col_count].astype(
                    jnp.float32
                )
                * depth_f,
                axis=(0, 1),
            )
        )
    tap_sums = jnp.stack(tap_list)
    spread_back = extend(depth_grad)
    padded = jnp.pad(spread_back, ((3, 3), (3, 3), (0, 0)))
    back_sum = jnp.zeros((row_count + 3, col_count, chan_count), jnp.float32)
    for tap in range(49):
        tap_row = tap // 7
        tap_col = tap % 7
        back_sum = (
            back_sum
            + padded[
                9 - tap_row : 12 - tap_row + row_count, 9 - tap_col : 9 - tap_col + col_count
            ].astype(jnp.float32)
            * taps[tap]
        )
    conv_grad = back_sum[:row_count]
    fold_grad = back_sum[row_count:].astype(jnp.bfloat16)
    own_index = lon_place * col_count + jnp.arange(col_count, dtype=jnp.int32)
    targets = jnp.take(mirror, own_index)
    every_grad = lax.all_gather(fold_grad, "lon", axis=1, tiled=True)
    picked = jnp.take(every_grad, targets, axis=1).astype(jnp.float32)
    lower_rows = conv_grad[row_count - 3 :] + jnp.where(north, picked[::-1], 0.0)
    total_grad = direct + jnp.concatenate([conv_grad[: row_count - 3], lower_rows], axis=0)
    grad_field = total_grad.astype(jnp.bfloat16)
    tap_sums, up_sums, down_sums, section_total = lax.psum(
        (tap_sums, up_sums, down_sums, section_total), ("lat", "lon")
    )
    return (
        level,
        grad_field,
        tap_sums * factor,
        up_sums * factor,
        down_sums * factor,
        section_total * factor,
    )


def solution(mesh):
    in_specs = (
        P("lat", "lon", None),
        P("lat", "lon"),
        P(),
        P(),
        P(),
        P(),
        P(),
        P(),
        P(),
        P(),
        P(),
        P(),
        P("lat", "lon", None),
    )
    out_specs = (P("lat", "lon", None), P("lat", "lon", None), P(), P(), P(), P())
    return jax.shard_map(
        on_device, mesh=mesh, in_specs=in_specs, out_specs=out_specs, check_vma=False
    )
```

profile of v0, /device:TPU:8, one launch (start us, length us, event | category | flops | bytes accessed | tf_op | source)
XLA Modules:
  0.0 652.1 jit_solution(4068497093461746249)
XLA Ops:
  8.6 2.0 collective-permute-start
  10.6 3.9 collective-permute-start.1
  16.0 1.5 gather_fusion
  33.6 3.2 collective-permute-start.2
  36.8 88.6 %all-gather.3.cloned.1.call-done = bf16[3,2048,128]{2,1,0:T(8,128)(2,1)} async-done(((bf16[3,32,128]{2,1,0:T(8,128)(2,1)}), bf16[3,2048,128]{2,1,0:T(8,128)(2,1)}) %all-gather.3.cloned.1.call-update) | async-done | bytes 1572880 | tf_op jit(solution)/shard_map/all_gather | solution.py:72
  125.3 3.2 copy.132
  130.8 22.6 %fusion.182 = (f32[128,32]{0,1:T(8,128)S(1)}, f32[128,32,128]{2,0,1:T(8,128)S(1)}) fusion(f32[128]{0:T(128)} %get-tuple-element.124, bf16[3,38,128]{2,0,1:T(4,128)(2,1)S(1)} %bitcast_select_fusion, bf16[128,38,128]{2,0,1:T(8,128)(2,1)S(1)} %get-tuple-element.122, f32[128]{0:T(128)} %get-tuple-element.125, f32[128]{0:T(128)} %get-tuple-element.126, ...), kind=kLoop, calls=%fused_computation.493 | loop fusion | flops 143126528 | bytes 10782208 | tf_op jit(solution)/shard_map/reduce_sum | solution.py:25
  156.9 4.6 multiply_convert_fusion
  163.4 4.1 convert_reduce_fusion
  176.5 1.5 copy.143
  179.3 1.6 copy.173
  180.9 1.7 reshape.462
  182.6 1.8 multiply_convert_fusion.4
  184.4 2.5 multiply_reduce_fusion.2
  188.2 3.5 fusion.12
  192.3 1.6 copy.148
  195.3 2.1 copy.149
  197.4 2.3 div.71
  199.7 7.5 %multiply_convert_fusion.2 = (bf16[128,32,128]{2,0,1:T(8,128)(2,1)S(1)}, bf16[128,32,128]{2,0,1:T(8,128)(2,1)}) fusion(f32[128]{0:T(128)} %convert_element_type.494, f32[128,32]{0,1:T(8,128)} %convert_element_type.492, f32[128,32]{0,1:T(8,128)} %broadcast_multiply_fusion.12, f32[128,32]{0,1:T(8,128)} %copy-done.36, bf16[128,32,128]{2,0,1:T(8,128)(2,1)} %copy-done.9, ...), kind=kLoop, calls=%fused_computation.273 | loop fusion | flops 6815744 | bytes 5325824 | tf_op jit(solution)/shard_map/convert_element_type | solution.py:135
  207.9 2.0 fusion.192
  209.9 6.9 %fusion.5 = bf16[4096,512]{1,0:T(8,128)(2,1)S(1)} fusion(f32[4096,512]{1,0:T(8,128)} %get-tuple-element.179, bf16[4096,128]{1,0:T(8,128)(2,1)S(1)} %bitcast.315, bf16[512,128]{1,0:T(8,128)(2,1)S(1)} %copy-done.49, f32[512]{0:T(512)S(1)} %copy-done.54), kind=kOutput, calls=%fused_computation.99 | convolution fusion | flops 559939584 | bytes 13764608 | tf_op jit(solution)/shard_map/dot_general | solution.py:137
  218.3 2.6 multiply_reduce_fusion.1
  221.1 3.7 multiply_reduce_fusion
  224.8 7.7 %fusion.113 = (f32[128]{0:T(128)}, f32[128]{0:T(128)}, f32[128]{0:T(128)}, f32[128]{0:T(128)}, f32[128]{0:T(128)}, /*index=5*/f32[128]{0:T(128)}, bf16[128,32,128]{2,0,1:T(8,128)(2,1)S(1)}) fusion(bf16[3,38,128]{2,0,1:T(4,128)(2,1)S(1)} %bitcast_select_fusion, bf16[128,38,128]{2,0,1:T(8,128)(2,1)S(1)} %get-tuple-element.122, ...), kind=kLoop, calls=%fused_computation.262 | loop fusion | flops 23592192 | bytes 6586368 | tf_op jit(solution)/shard_map/reduce_sum | solution.py:152
  232.6 4.1 fusion.114
  236.6 2.0 fusion.94
  239.3 1.6 copy.155
  242.2 1.8 convolution_bitcast_fusion.4
  245.4 1.6 collective-permute-start.4
  247.0 2.6 collective-permute-start.5
  249.6 3.2 fusion.85
  252.9 4.1 fusion.87
  260.8 1.5 collective-permute-done.7
  263.4 1.8 pad_maximum_fusion.1
  265.6 20.2 %multiply_add_fusion = f32[131,32,128]{2,0,1:T(8,128)S(1)} fusion(bf16[131,38,128]{2,0,1:T(8,128)(2,1)S(1)} %get-tuple-element.102, bf16[134,38,128]{2,0,1:T(8,128)(2,1)S(1)} %pad_maximum_fusion, bf16[131,38,128]{2,0,1:T(8,128)(2,1)S(1)} %get-tuple-element.101, f32[128]{0:T(128)S(1)} %copy-done.79, f32[128]{0:T(128)S(1)} %copy-done.80, ...), kind=kLoop, calls=%fused_computation.159 | loop fusion | flops 78340096 | bytes 34689536 | tf_op jit(solution)/shard_map/add | solution.py:168
  289.2 2.8 fusion.86
  292.0 3.4 fusion.112
  295.7 4.0 fusion.115
  300.1 78.6 %psum.28 = f32[49,128]{1,0:T(8,128)S(1)} all-reduce(f32[49,128]{1,0:T(8,128)S(1)} %stack.202), channel_id=1, replica_groups=mesh['lat'=4,'lon'=64] {'lat','lon'}, use_global_device_ids=true, to_apply=%region_65.66 | all-reduce | flops 6272 | bytes 50176 | tf_op jit(solution)/shard_map/psum | solution.py:183
  379.3 143.9 %all-reduce.4.cloned.1.call-done = (f32[128,512]{1,0:T(8,128)}, f32[512,128]{1,0:T(8,128)}, f32[3,512,128]{2,1,0:T(8,128)}) async-done(((f32[128,512]{1,0:T(8,128)}, f32[512,128]{1,0:T(8,128)}, f32[3,512,128]{2,1,0:T(8,128)}), (f32[128,512]{1,0:T(8,128)}, f32[512,128]{1,0:T(8,128)}, f32[3,512,128]{2,1,0:T(8,128)})) %all-reduce.4.cloned.1.call-update) | async-done | bytes 1310736 | tf_op jit(solution)/shard_map/psum | solution.py:183
  523.2 1.7 broadcast_multiply_fusion.1
  524.9 1.7 broadcast_multiply_fusion.2
  526.6 2.1 broadcast_multiply_fusion
  528.6 105.6 %all-gather.5.cloned.1.call-done = bf16[3,2048,128]{2,1,0:T(8,128)(2,1)} async-done(((bf16[3,32,128]{2,1,0:T(8,128)(2,1)}), bf16[3,2048,128]{2,1,0:T(8,128)(2,1)}) %all-gather.5.cloned.1.call-update) | async-done | bytes 1572880 | tf_op jit(solution)/shard_map/all_gather | solution.py:178
  634.2 4.2 copy.154
  638.4 2.3 gather_fusion.3
  641.9 1.8 fusion.116
  643.7 1.6 copy.162
  (401 shorter events, 55.0 us)
Async XLA Ops:
  7.2 149.7 %copy-start = (bf16[128,512]{1,0:T(8,128)(2,1)S(1)}, bf16[128,512]{1,0:T(8,128)(2,1)}, u32[]{:S(2)}) copy-start(bf16[128,512]{1,0:T(8,128)(2,1)} %param.18) | copy-start | bytes 393220
  7.2 17.7 %copy-start.12 = (bf16[128,32,128]{2,1,0:T(8,128)(2,1)S(1)}, bf16[128,32,128]{2,1,0:T(8,128)(2,1)}, u32[]{:S(2)}) copy-start(bf16[128,32,128]{2,1,0:T(8,128)(2,1)} %param.13) | copy-start | bytes 3145732
  7.2 12.3 %copy-start.58 = (bf16[49,128]{1,0:T(8,128)(2,1)S(1)}, bf16[49,128]{1,0:T(8,128)(2,1)}, u32[]{:S(2)}) copy-start(bf16[49,128]{1,0:T(8,128)(2,1)} %param.16) | copy-start | bytes 37636
  7.2 12.9 %copy-start.106 = (bf16[3,128]{1,0:T(4,128)(2,1)S(1)}, bf16[3,128]{1,0:T(4,128)(2,1)}, u32[]{:S(2)}) copy-start(bf16[3,128]{1,0:T(4,128)(2,1)} %param.22) | copy-start | bytes 2308
  7.2 13.5 %copy-start.107 = (bf16[3,128]{1,0:T(4,128)(2,1)S(1)}, bf16[3,128]{1,0:T(4,128)(2,1)}, u32[]{:S(2)}) copy-start(bf16[3,128]{1,0:T(4,128)(2,1)} %param.24) | copy-start | bytes 2308
  7.2 16.0 %copy-start.38 = (bf16[3,512,128]{2,1,0:T(8,128)(2,1)S(1)}, bf16[3,512,128]{2,1,0:T(8,128)(2,1)}, u32[]{:S(2)}) copy-start(bf16[3,512,128]{2,1,0:T(8,128)(2,1)} %param.23) | copy-start | bytes 1179652
  7.2 16.7 %copy-start.55 = (bf16[16,4,128]{2,1,0:T(4,128)(2,1)S(1)}, bf16[16,4,128]{2,1,0:T(4,128)(2,1)}, u32[]{:S(2)}) copy-start(bf16[16,4,128]{2,1,0:T(4,128)(2,1)} %param.25) | copy-start | bytes 49156
  7.2 118.1 %all-gather.3.cloned.1.call-start = ((), (), s32[]{:S(2)}) async-start(), calls=%async_computation | async-start | bytes 1597440 | tf_op jit(solution)/shard_map/all_gather | solution.py:72
  8.6 16.2 %collective-permute-start = (bf16[128,3,128]{2,0,1:T(8,128)(2,1)S(1)}, bf16[128,3,128]{2,0,1:T(8,128)(2,1)S(1)}, u32[]{:S(2)}, u32[]{:S(2)}) collective-permute-start(bf16[128,3,128]{2,0,1:T(8,128)(2,1)S(1)} %copy.210), channel_id=1, source_target_pairs={{0,1},{1,2},{2,3},{3,4},{4,5},{5,6},{6,7},{7,8},{8,9},{9,10},{10,1... | collective-permute-start | bytes 294920 | tf_op jit(solution)/shard_map/ppermute | solution.py:18
  10.6 15.1 %collective-permute-start.1 = (bf16[128,3,128]{2,0,1:T(8,128)(2,1)S(1)}, bf16[128,3,128]{2,0,1:T(8,128)(2,1)S(1)}, u32[]{:S(2)}, u32[]{:S(2)}) collective-permute-start(bf16[128,3,128]{2,0,1:T(8,128)(2,1)S(1)} %copy.209), channel_id=1, source_target_pairs={{1,0},{2,1},{3,2},{4,3},{5,4},{6,5},{7,6},{8,7},{9,8},{10,9},{11,1... | collective-permute-start | bytes 294920 | tf_op jit(solution)/shard_map/ppermute | solution.py:19
  15.9 507.3 %all-reduce.4.cloned.1.call-start = ((), (), s32[]{:S(2)}) async-start(), calls=%async_computation.2 | async-start | bytes 2621440 | tf_op jit(solution)/shard_map/psum | solution.py:183
  24.9 4.8 copy-start.143
  24.9 5.3 copy-start.140
  24.9 5.9 copy-start.57
  24.9 6.5 copy-start.144
  27.8 102.1 %collective-permute-start.3 = (bf16[3,38,128]{2,0,1:T(4,128)(2,1)S(1)}, bf16[3,38,128]{2,0,1:T(4,128)(2,1)}, u32[]{:S(2)}, u32[]{:S(2)}) collective-permute-start(bf16[3,38,128]{2,0,1:T(4,128)(2,1)S(1)} %get-tuple-element.106), channel_id=1, source_target_pairs={{64,0},{128,64},{192,128},{65,1},{129,65},{193,129},{66,2},{130,66... | collective-permute-start | bytes 87560 | tf_op jit(solution)/shard_map/ppermute | solution.py:19
  33.6 97.3 %collective-permute-start.2 = (bf16[3,38,128]{2,0,1:T(4,128)(2,1)}, bf16[3,38,128]{2,0,1:T(4,128)(2,1)S(1)}, u32[]{:S(2)}, u32[]{:S(2)}) collective-permute-start(bf16[3,38,128]{2,0,1:T(4,128)(2,1)} %get-tuple-element.105), channel_id=1, source_target_pairs={{0,64},{64,128},{128,192},{1,65},{65,129},{129,193},{2,66},{66,130... | collective-permute-start | bytes 87560 | tf_op jit(solution)/shard_map/ppermute | solution.py:18
  153.5 67.6 %copy-start.4 = (f32[128,32,128]{2,0,1:T(8,128)}, f32[128,32,128]{2,0,1:T(8,128)S(1)}, u32[]{:S(2)}) copy-start(f32[128,32,128]{2,0,1:T(8,128)S(1)} %get-tuple-element.100) | copy-start | bytes 6291460
  156.8 4.6 copy-start.16
  156.9 4.6 copy-start.48
  163.4 5.5 copy-start.63
  199.7 8.2 %copy-start.3 = (bf16[4096,512]{1,0:T(8,128)(2,1)S(1)}, bf16[4096,512]{1,0:T(8,128)(2,1)}, u32[]{:S(2)}) copy-start(bf16[4096,512]{1,0:T(8,128)(2,1)} %copy-done.2) | copy-start | bytes 12582916
  209.9 6.9 %copy-start.17 = (bf16[128,32,128]{2,1,0:T(8,128)(2,1)S(1)}, bf16[128,32,128]{2,1,0:T(8,128)(2,1)}, u32[]{:S(2)}) copy-start(bf16[128,32,128]{2,1,0:T(8,128)(2,1)} %copy-done.16) | copy-start | bytes 3145732
  242.2 4.8 copy-start.50
  245.4 11.7 %collective-permute-start.4 = (bf16[128,3,128]{2,0,1:T(8,128)(2,1)S(1)}, bf16[128,3,128]{2,0,1:T(8,128)(2,1)S(1)}, u32[]{:S(2)}, u32[]{:S(2)}) collective-permute-start(bf16[128,3,128]{2,0,1:T(8,128)(2,1)S(1)} %copy-done.51), channel_id=1, source_target_pairs={{0,1},{1,2},{2,3},{3,4},{4,5},{5,6},{6,7},{7,8},{8,9},{9,10},{10,1... | collective-permute-start | bytes 294920 | tf_op jit(solution)/shard_map/ppermute | solution.py:18
  247.0 9.9 %copy-start.56 = (bf16[16,4,128]{2,1,0:T(4,128)(2,1)S(1)}, bf16[16,4,128]{2,1,0:T(4,128)(2,1)}, u32[]{:S(2)}) copy-start(bf16[16,4,128]{2,1,0:T(4,128)(2,1)} %param.25) | copy-start | bytes 49156
  247.0 10.1 %collective-permute-start.5 = (bf16[128,3,128]{2,0,1:T(8,128)(2,1)S(1)}, bf16[128,3,128]{2,0,1:T(8,128)(2,1)S(1)}, u32[]{:S(2)}, u32[]{:S(2)}) collective-permute-start(bf16[128,3,128]{2,0,1:T(8,128)(2,1)S(1)} %copy-done.50), channel_id=1, source_target_pairs={{1,0},{2,1},{3,2},{4,3},{5,4},{6,5},{7,6},{8,7},{9,8},{10,9},{11,1... | collective-permute-start | bytes 294920 | tf_op jit(solution)/shard_map/ppermute | solution.py:19
  252.8 6.9 %copy-start.45 = (f32[1,512,128]{2,1,0:T(8,128)S(1)}, f32[1,512,128]{2,1,0:T(8,128)}, u32[]{:S(2)}) copy-start(f32[1,512,128]{2,1,0:T(8,128)} %convolution_bitcast_fusion.3) | copy-start | bytes 786436
  257.2 3.7 collective-permute-start.6
  258.5 3.9 collective-permute-start.7
  260.8 373.4 %all-gather.5.cloned.1.call-start = ((), (), s32[]{:S(2)}) async-start(), calls=%async_computation.1 | async-start | bytes 1597440 | tf_op jit(solution)/shard_map/all_gather | solution.py:178
  265.6 22.2 %copy-start.27 = (bf16[1,512,128]{2,1,0:T(8,128)(2,1)S(1)}, bf16[1,512,128]{2,1,0:T(8,128)(2,1)}, u32[]{:S(2)}) copy-start(bf16[1,512,128]{2,1,0:T(8,128)(2,1)} %copy-done.26) | copy-start | bytes 393220
  289.2 6.2 copy-start.14
  295.4 4.3 copy-start.108
  295.4 4.3 copy-start.109
  295.4 4.3 copy-start.110
  295.4 4.3 copy-start.111
  295.4 4.3 copy-start.112
  295.4 4.3 copy-start.113
  295.4 4.3 copy-start.114
  295.4 4.3 copy-start.115
  295.4 4.3 copy-start.116
  295.5 4.3 copy-start.117
  295.5 4.3 copy-start.118
  295.5 4.3 copy-start.119
  528.6 112.1 %copy-start.141 = (pred[32]{0:T(512)(128)(4,1)S(1)}, pred[32]{0:T(512)(128)(4,1)}, u32[]{:S(2)}) copy-start(pred[32]{0:T(512)(128)(4,1)} %compare_and_fusion) | copy-start | bytes 100
  528.6 113.2 %slice-start = ((f32[131,32,128]{2,0,1:T(8,128)}), f32[125,32,128]{2,0,1:T(8,128)S(1)}, s32[]{:S(2)}) async-start(f32[131,32,128]{2,0,1:T(8,128)} %copy-done.18), calls=%async_computation.3 | async-start | bytes 4194304 | tf_op jit(solution)/shard_map/slice | solution.py:181
  528.6 113.2 %copy-start.40 = (f32[128,32]{0,1:T(8,128)S(1)}, f32[128,32]{0,1:T(8,128)}, u32[]{:S(2)}) copy-start(f32[128,32]{0,1:T(8,128)} %convert_element_type.492) | copy-start | bytes 49156
  (109 other events, 290.4 us)
Sparse Core Ops, SparseCore 0:
  16.0 109.2 all-gather.2
  260.9 262.2 all-reduce.3
  526.7 107.4 all-gather.4
where the time goes:
time: 657 us; the launch traced here: 652 us
  waiting for transfers between devices  340 us (52%)
  other arithmetic  125 us (19%)
  blocking collectives  78.6 us (12%)
  local copies, waits for them, and re-layouts  47.4 us (7%)
  matrix products  27.5 us (4%)
  starting transfers between devices  17.3 us (3%)
  between operations  16.4 us (2%)
    psum x1, waiting for transfers between devices, on_device(): lax.psum((tap_sums, up_sums, down_sums, section_total), ('lat', 'lon'))  144 us
    all_gather x1, waiting for transfers between devices, on_device(): every_grad = lax.all_gather(fold_grad, 'lon', axis=1, tiled=True)  106 us
    all_gather x1, waiting for transfers between devices, on_device(): every_top = lax.all_gather(top_rows, 'lon', axis=1, tiled=True)  88.6 us
    psum x1, blocking collectives, on_device(): lax.psum((tap_sums, up_sums, down_sums, section_total), ('lat', 'lon'))  78.6 us
    reduce_sum x8, other arithmetic, on_device(): jnp.sum(extended[tap_row:tap_row + row_count, tap_col:tap_col + col_count...  31.3 us
    reduce_sum x2, other arithmetic, norm_parts(): center = values - jnp.mean(values, axis=-1, keepdims=True)  26.7 us
    add x1, other arithmetic, on_device(): back_sum + padded[9 - tap_row:12 - tap_row + row_count, 9 - tap_col:9 - t...  20.2 us
  transfers between devices with their start and end apart: 11, of which 4 were waited for; matrix products, arithmetic and copies ran while one was open for 11% of the time, Pallas kernels for 0%

commit v1 on v0

--- a/solution.py
+++ b/solution.py
@@ -175,7 +175,8 @@
     fold_grad = back_sum[row_count:].astype(jnp.bfloat16)
     own_index = lon_place * col_count + jnp.arange(col_count, dtype=jnp.int32)
     targets = jnp.take(mirror, own_index)
-    every_grad = lax.all_gather(fold_grad, "lon", axis=1, tiled=True)
+    repeated = jnp.stack([fold_grad] * lax.axis_size("lon"))
+    every_grad = jnp.concatenate(lax.all_to_all(repeated, "lon", 0, 0), axis=1)
     picked = jnp.take(every_grad, targets, axis=1).astype(jnp.float32)
     lower_rows = conv_grad[row_count - 3 :] + jnp.where(north, picked[::-1], 0.0)
     total_grad = direct + jnp.concatenate([conv_grad[: row_count - 3], lower_rows], axis=0)

time: 657 us -> 547 us (0.83)
  waiting for transfers between devices: 340 us -> 208 us
  local copies, waits for them, and re-layouts: 47.4 us -> 58.1 us
  starting transfers between devices: 17.3 us -> 27.3 us
    all_gather x1 -> x0, waiting for transfers between devices: 106 us -> none  [on_device(): every_grad = lax.all_gather(fold_grad, 'lon', axis=1, tiled=True)]
    psum x1, waiting for transfers between devices: 144 us -> 118 us  [on_device(): lax.psum((tap_sums, up_sums, down_sums, section_total), ('lat', 'lon'))]
    reshape x0 -> x1, local copies, waits for them, and re-layouts: none -> 10.7 us  [on_device(): every_grad = jnp.concatenate(lax.all_to_all(repeated, 'lon', 0, 0), axis=1)]
    all_to_all x0 -> x1, starting transfers between devices: none -> 9.85 us  [on_device(): every_grad = jnp.concatenate(lax.all_to_all(repeated, 'lon', 0, 0), axis=1)]
  transfers between devices with their start and end apart: 11 -> 11, of which waited for: 4 -> 3; matrix products, arithmetic and copies ran while one was open for 11% -> 14% of each run, Pallas kernels for 0% -> 0%
where the time goes in v1:
time: 547 us; the launch traced here: 542 us
  waiting for transfers between devices  208 us (38%)
  other arithmetic  123 us (22%)
  blocking collectives  80.8 us (15%)
  local copies, waits for them, and re-layouts  58.1 us (11%)
  matrix products  27.6 us (5%)
  starting transfers between devices  27.3 us (5%)
  between operations  16.5 us (3%)
    psum x1, waiting for transfers between devices, on_device(): lax.psum((tap_sums, up_sums, down_sums, section_total), ('lat', 'lon'))  118 us
    all_gather x1, waiting for transfers between devices, on_device(): every_top = lax.all_gather(top_rows, 'lon', axis=1, tiled=True)  88.6 us
    psum x1, blocking collectives, on_device(): lax.psum((tap_sums, up_sums, down_sums, section_total), ('lat', 'lon'))  80.8 us
    reduce_sum x8, other arithmetic, on_device(): jnp.sum(extended[tap_row:tap_row + row_count, tap_col:tap_col + col_count...  29.3 us
    reduce_sum x2, other arithmetic, norm_parts(): center = values - jnp.mean(values, axis=-1, keepdims=True)  26.7 us
    add x1, other arithmetic, on_device(): back_sum + padded[9 - tap_row:12 - tap_row + row_count, 9 - tap_col:9 - t...  20.5 us
  transfers between devices with their start and end apart: 11, of which 3 were waited for; matrix products, arithmetic and copies ran while one was open for 14% of the time, Pallas kernels for 0%

profile of v1, /device:TPU:8, one launch (start us, length us, event | category | flops | bytes accessed | tf_op | source)
XLA Modules:
  0.0 541.9 jit_solution(9116973558509474068)
XLA Ops:
  8.6 2.0 collective-permute-start
  10.6 3.9 collective-permute-start.1
  33.6 3.2 collective-permute-start.2
  36.8 88.6 %all-gather.2.cloned.1.call-done = bf16[3,2048,128]{2,1,0:T(8,128)(2,1)} async-done(((bf16[3,32,128]{2,1,0:T(8,128)(2,1)}), bf16[3,2048,128]{2,1,0:T(8,128)(2,1)}) %all-gather.2.cloned.1.call-update) | async-done | bytes 1572880 | tf_op jit(solution)/shard_map/all_gather | solution.py:72
  125.3 3.2 copy.137
  130.8 22.6 %fusion.182 = (f32[128,32]{0,1:T(8,128)S(1)}, f32[128,32,128]{2,0,1:T(8,128)S(1)}) fusion(f32[128]{0:T(128)} %get-tuple-element.124, bf16[3,38,128]{2,0,1:T(4,128)(2,1)S(1)} %bitcast_select_fusion, bf16[128,38,128]{2,0,1:T(8,128)(2,1)S(1)} %get-tuple-element.122, f32[128]{0:T(128)} %get-tuple-element.125, f32[128]{0:T(128)} %get-tuple-element.126, ...), kind=kLoop, calls=%fused_computation.493 | loop fusion | flops 143126528 | bytes 10782208 | tf_op jit(solution)/shard_map/reduce_sum | solution.py:25
  156.9 4.6 multiply_convert_fusion
  163.4 4.1 convert_reduce_fusion
  176.5 1.5 copy.148
  179.3 1.6 copy.179
  180.9 1.7 reshape.472
  182.6 1.8 multiply_convert_fusion.4
  184.4 2.5 multiply_reduce_fusion.2
  188.2 3.5 fusion.12
  192.3 1.6 copy.153
  195.3 2.1 copy.154
  197.4 2.3 div.71
  199.7 7.5 %multiply_convert_fusion.2 = (bf16[128,32,128]{2,0,1:T(8,128)(2,1)S(1)}, bf16[128,32,128]{2,0,1:T(8,128)(2,1)}) fusion(f32[128]{0:T(128)} %convert_element_type.494, f32[128,32]{0,1:T(8,128)} %convert_element_type.492, f32[128,32]{0,1:T(8,128)} %broadcast_multiply_fusion.12, f32[128,32]{0,1:T(8,128)} %copy-done.37, bf16[128,32,128]{2,0,1:T(8,128)(2,1)} %copy-done.9, ...), kind=kLoop, calls=%fused_computation.273 | loop fusion | flops 6815744 | bytes 5325824 | tf_op jit(solution)/shard_map/convert_element_type | solution.py:135
  207.9 2.0 fusion.192
  209.9 6.9 %fusion.5 = bf16[4096,512]{1,0:T(8,128)(2,1)S(1)} fusion(f32[4096,512]{1,0:T(8,128)} %get-tuple-element.179, bf16[4096,128]{1,0:T(8,128)(2,1)S(1)} %bitcast.319, bf16[512,128]{1,0:T(8,128)(2,1)S(1)} %copy-done.49, f32[512]{0:T(512)S(1)} %copy-done.54), kind=kOutput, calls=%fused_computation.99 | convolution fusion | flops 559939584 | bytes 13764608 | tf_op jit(solution)/shard_map/dot_general | solution.py:137
  218.3 2.6 multiply_reduce_fusion.1
  221.1 3.7 multiply_reduce_fusion
  224.8 7.7 %fusion.113 = (f32[128]{0:T(128)}, f32[128]{0:T(128)}, f32[128]{0:T(128)}, f32[128]{0:T(128)}, f32[128]{0:T(128)}, /*index=5*/f32[128]{0:T(128)}, bf16[128,32,128]{2,0,1:T(8,128)(2,1)S(1)}) fusion(bf16[3,38,128]{2,0,1:T(4,128)(2,1)S(1)} %bitcast_select_fusion, bf16[128,38,128]{2,0,1:T(8,128)(2,1)S(1)} %get-tuple-element.122, ...), kind=kLoop, calls=%fused_computation.262 | loop fusion | flops 23592192 | bytes 6586368 | tf_op jit(solution)/shard_map/reduce_sum | solution.py:152
  232.6 4.1 fusion.114
  237.3 1.6 copy.161
  240.2 1.8 convolution_bitcast_fusion.4
  244.3 1.6 collective-permute-start.4
  246.0 2.6 collective-permute-start.5
  248.5 1.9 pad_maximum_fusion.4
  250.4 2.5 fusion.85
  253.0 2.8 fusion.86
  259.4 1.6 collective-permute-done.7
  262.0 1.8 pad_maximum_fusion.1
  264.2 20.5 %multiply_add_fusion = f32[131,32,128]{2,0,1:T(8,128)S(1)} fusion(bf16[131,38,128]{2,0,1:T(8,128)(2,1)S(1)} %get-tuple-element.102, bf16[134,38,128]{2,0,1:T(8,128)(2,1)S(1)} %pad_maximum_fusion, bf16[131,38,128]{2,0,1:T(8,128)(2,1)S(1)} %get-tuple-element.101, f32[128]{0:T(128)S(1)} %copy-done.78, f32[128]{0:T(128)S(1)} %copy-done.79, ...), kind=kLoop, calls=%fused_computation.159 | loop fusion | flops 78340096 | bytes 34689536 | tf_op jit(solution)/shard_map/add | solution.py:168
  287.5 9.8 %all-to-all-start = ((bf16[64,3,32,128]{3,2,1,0:T(8,128)(2,1)}), bf16[64,3,32,128]{3,2,1,0:T(8,128)(2,1)}, u32[]{:S(2)}, u32[]{:S(2)}) async-start(bf16[64,3,32,128]{3,2,1,0:T(8,128)(2,1)} %stack.104), calls=%async_computation | async-start | bytes 3145728 | tf_op jit(solution)/shard_map/all_to_all | solution.py:179
  297.4 3.5 fusion.87
  300.8 3.4 fusion.112
  304.2 4.0 fusion.115
  310.1 80.8 %psum.28 = f32[49,128]{1,0:T(8,128)S(1)} all-reduce(f32[49,128]{1,0:T(8,128)S(1)} %stack.270), channel_id=1, replica_groups=mesh['lat'=4,'lon'=64] {'lat','lon'}, use_global_device_ids=true, to_apply=%region_65.66 | all-reduce | flops 6272 | bytes 50176 | tf_op jit(solution)/shard_map/psum | solution.py:184
  391.5 1.7 slice.1018
  393.2 117.9 %all-reduce.4.cloned.1.call-done = (f32[128,512]{1,0:T(8,128)}, f32[512,128]{1,0:T(8,128)}, f32[3,512,128]{2,1,0:T(8,128)}) async-done(((f32[128,512]{1,0:T(8,128)}, f32[512,128]{1,0:T(8,128)}, f32[3,512,128]{2,1,0:T(8,128)}), (f32[128,512]{1,0:T(8,128)}, f32[512,128]{1,0:T(8,128)}, f32[3,512,128]{2,1,0:T(8,128)})) %all-reduce.4.cloned.1.call-update) | async-done | bytes 1310736 | tf_op jit(solution)/shard_map/psum | solution.py:184
  511.1 1.7 broadcast_multiply_fusion.1
  512.8 1.7 broadcast_multiply_fusion.2
  514.4 2.1 broadcast_multiply_fusion
  516.5 1.7 copy.159
  518.2 10.7 %copy.160 = bf16[3,2048,128]{2,0,1:T(4,128)(2,1)} copy(bf16[3,2048,128]{2,1,0:T(8,128)(2,1)S(1)} %bitcast.313) | data formatting | bytes 3145728 | tf_op jit(solution)/shard_map/reshape | solution.py:179
  529.0 2.3 gather_fusion.3
  533.2 1.6 copy.168
  (367 shorter events, 58.5 us)
Async XLA Ops:
  7.2 149.7 %copy-start = (bf16[128,512]{1,0:T(8,128)(2,1)S(1)}, bf16[128,512]{1,0:T(8,128)(2,1)}, u32[]{:S(2)}) copy-start(bf16[128,512]{1,0:T(8,128)(2,1)} %param.18) | copy-start | bytes 393220
  7.2 17.7 %copy-start.12 = (bf16[128,32,128]{2,1,0:T(8,128)(2,1)S(1)}, bf16[128,32,128]{2,1,0:T(8,128)(2,1)}, u32[]{:S(2)}) copy-start(bf16[128,32,128]{2,1,0:T(8,128)(2,1)} %param.13) | copy-start | bytes 3145732
  7.2 12.3 %copy-start.57 = (bf16[49,128]{1,0:T(8,128)(2,1)S(1)}, bf16[49,128]{1,0:T(8,128)(2,1)}, u32[]{:S(2)}) copy-start(bf16[49,128]{1,0:T(8,128)(2,1)} %param.16) | copy-start | bytes 37636
  7.2 12.9 %copy-start.106 = (bf16[3,128]{1,0:T(4,128)(2,1)S(1)}, bf16[3,128]{1,0:T(4,128)(2,1)}, u32[]{:S(2)}) copy-start(bf16[3,128]{1,0:T(4,128)(2,1)} %param.22) | copy-start | bytes 2308
  7.2 13.5 %copy-start.107 = (bf16[3,128]{1,0:T(4,128)(2,1)S(1)}, bf16[3,128]{1,0:T(4,128)(2,1)}, u32[]{:S(2)}) copy-start(bf16[3,128]{1,0:T(4,128)(2,1)} %param.24) | copy-start | bytes 2308
  7.2 15.9 %copy-start.39 = (bf16[3,512,128]{2,1,0:T(8,128)(2,1)S(1)}, bf16[3,512,128]{2,1,0:T(8,128)(2,1)}, u32[]{:S(2)}) copy-start(bf16[3,512,128]{2,1,0:T(8,128)(2,1)} %param.23) | copy-start | bytes 1179652
  7.2 16.7 %copy-start.55 = (bf16[16,4,128]{2,1,0:T(4,128)(2,1)S(1)}, bf16[16,4,128]{2,1,0:T(4,128)(2,1)}, u32[]{:S(2)}) copy-start(bf16[16,4,128]{2,1,0:T(4,128)(2,1)} %param.25) | copy-start | bytes 49156
  7.2 118.1 %all-gather.2.cloned.1.call-start = ((), (), s32[]{:S(2)}) async-start(), calls=%async_computation.1 | async-start | bytes 1597440 | tf_op jit(solution)/shard_map/all_gather | solution.py:72
  8.6 16.2 %collective-permute-start = (bf16[128,3,128]{2,0,1:T(8,128)(2,1)S(1)}, bf16[128,3,128]{2,0,1:T(8,128)(2,1)S(1)}, u32[]{:S(2)}, u32[]{:S(2)}) collective-permute-start(bf16[128,3,128]{2,0,1:T(8,128)(2,1)S(1)} %copy.216), channel_id=1, source_target_pairs={{0,1},{1,2},{2,3},{3,4},{4,5},{5,6},{6,7},{7,8},{8,9},{9,10},{10,1... | collective-permute-start | bytes 294920 | tf_op jit(solution)/shard_map/ppermute | solution.py:18
  10.6 15.1 %collective-permute-start.1 = (bf16[128,3,128]{2,0,1:T(8,128)(2,1)S(1)}, bf16[128,3,128]{2,0,1:T(8,128)(2,1)S(1)}, u32[]{:S(2)}, u32[]{:S(2)}) collective-permute-start(bf16[128,3,128]{2,0,1:T(8,128)(2,1)S(1)} %copy.215), channel_id=1, source_target_pairs={{1,0},{2,1},{3,2},{4,3},{5,4},{6,5},{7,6},{8,7},{9,8},{10,9},{11,1... | collective-permute-start | bytes 294920 | tf_op jit(solution)/shard_map/ppermute | solution.py:19
  15.9 495.2 %all-reduce.4.cloned.1.call-start = ((), (), s32[]{:S(2)}) async-start(), calls=%async_computation.2 | async-start | bytes 2621440 | tf_op jit(solution)/shard_map/psum | solution.py:184
  20.7 4.1 copy-start.64
  24.9 4.8 copy-start.126
  24.9 5.3 copy-start.123
  24.9 5.9 %copy-start.56 = (s32[128,32]{0,1:T(8,128)S(1)}, s32[128,32]{0,1:T(8,128)}, u32[]{:S(2)}) copy-start(s32[128,32]{0,1:T(8,128)} %param.14) | copy-start | bytes 49156
  24.9 6.5 %copy-start.127 = (bf16[128]{0:T(256)(128)(2,1)S(1)}, bf16[128]{0:T(256)(128)(2,1)}, u32[]{:S(2)}) copy-start(bf16[128]{0:T(256)(128)(2,1)} %param.21) | copy-start | bytes 772
  27.8 102.1 %collective-permute-start.3 = (bf16[3,38,128]{2,0,1:T(4,128)(2,1)S(1)}, bf16[3,38,128]{2,0,1:T(4,128)(2,1)}, u32[]{:S(2)}, u32[]{:S(2)}) collective-permute-start(bf16[3,38,128]{2,0,1:T(4,128)(2,1)S(1)} %get-tuple-element.106), channel_id=1, source_target_pairs={{64,0},{128,64},{192,128},{65,1},{129,65},{193,129},{66,2},{130,66... | collective-permute-start | bytes 87560 | tf_op jit(solution)/shard_map/ppermute | solution.py:19
  33.6 97.3 %collective-permute-start.2 = (bf16[3,38,128]{2,0,1:T(4,128)(2,1)}, bf16[3,38,128]{2,0,1:T(4,128)(2,1)S(1)}, u32[]{:S(2)}, u32[]{:S(2)}) collective-permute-start(bf16[3,38,128]{2,0,1:T(4,128)(2,1)} %get-tuple-element.105), channel_id=1, source_target_pairs={{0,64},{64,128},{128,192},{1,65},{65,129},{129,193},{2,66},{66,130... | collective-permute-start | bytes 87560 | tf_op jit(solution)/shard_map/ppermute | solution.py:18
  153.5 67.6 %copy-start.4 = (f32[128,32,128]{2,0,1:T(8,128)}, f32[128,32,128]{2,0,1:T(8,128)S(1)}, u32[]{:S(2)}) copy-start(f32[128,32,128]{2,0,1:T(8,128)S(1)} %get-tuple-element.100) | copy-start | bytes 6291460
  156.8 4.6 copy-start.16
  156.9 4.6 copy-start.48
  163.4 5.5 %copy-start.62 = (f32[128]{0:T(128)S(1)}, f32[128]{0:T(128)}, u32[]{:S(2)}) copy-start(f32[128]{0:T(128)} %get-tuple-element.176) | copy-start | bytes 1540
  167.5 3.8 copy-start.9
  171.3 3.8 copy-start.19
  171.3 3.7 copy-start.31
  188.2 3.5 copy-start.15
  199.7 8.2 %copy-start.3 = (bf16[4096,512]{1,0:T(8,128)(2,1)S(1)}, bf16[4096,512]{1,0:T(8,128)(2,1)}, u32[]{:S(2)}) copy-start(bf16[4096,512]{1,0:T(8,128)(2,1)} %copy-done.2) | copy-start | bytes 12582916
  209.9 6.9 %copy-start.17 = (bf16[128,32,128]{2,1,0:T(8,128)(2,1)S(1)}, bf16[128,32,128]{2,1,0:T(8,128)(2,1)}, u32[]{:S(2)}) copy-start(bf16[128,32,128]{2,1,0:T(8,128)(2,1)} %copy-done.16) | copy-start | bytes 3145732
  221.1 3.7 copy-start.11
  221.1 3.7 copy-start.36
  221.1 3.7 copy-start.43
  221.1 3.7 copy-start.61
  232.6 4.8 copy-start.22
  240.2 4.1 copy-start.51
  240.2 5.7 %copy-start.50 = (bf16[128,3,128]{2,0,1:T(8,128)(2,1)S(1)}, bf16[128,3,128]{2,0,1:T(8,128)(2,1)}, u32[]{:S(2)}) copy-start(bf16[128,3,128]{2,0,1:T(8,128)(2,1)} %get-tuple-element.108) | copy-start | bytes 294916
  244.3 11.4 %collective-permute-start.4 = (bf16[128,3,128]{2,0,1:T(8,128)(2,1)S(1)}, bf16[128,3,128]{2,0,1:T(8,128)(2,1)S(1)}, u32[]{:S(2)}, u32[]{:S(2)}) collective-permute-start(bf16[128,3,128]{2,0,1:T(8,128)(2,1)S(1)} %copy-done.51), channel_id=1, source_target_pairs={{0,1},{1,2},{2,3},{3,4},{4,5},{5,6},{6,7},{7,8},{8,9},{9,10},{10,1... | collective-permute-start | bytes 294920 | tf_op jit(solution)/shard_map/ppermute | solution.py:18
  246.0 9.8 %collective-permute-start.5 = (bf16[128,3,128]{2,0,1:T(8,128)(2,1)S(1)}, bf16[128,3,128]{2,0,1:T(8,128)(2,1)S(1)}, u32[]{:S(2)}, u32[]{:S(2)}) collective-permute-start(bf16[128,3,128]{2,0,1:T(8,128)(2,1)S(1)} %copy-done.50), channel_id=1, source_target_pairs={{1,0},{2,1},{3,2},{4,3},{5,4},{6,5},{7,6},{8,7},{9,8},{10,9},{11,1... | collective-permute-start | bytes 294920 | tf_op jit(solution)/shard_map/ppermute | solution.py:19
  252.9 5.7 %copy-start.28 = (bf16[1,512,128]{2,1,0:T(8,128)(2,1)S(1)}, bf16[1,512,128]{2,1,0:T(8,128)(2,1)}, u32[]{:S(2)}) copy-start(bf16[1,512,128]{2,1,0:T(8,128)(2,1)} %copy-done.27) | copy-start | bytes 393220
  253.0 5.7 %copy-start.115 = (f32[128]{0:T(128)S(1)}, f32[128]{0:T(128)}, u32[]{:S(2)}) copy-start(f32[128]{0:T(128)} %get-tuple-element.172) | copy-start | bytes 1540
  255.8 3.6 collective-permute-start.6
  257.1 3.9 collective-permute-start.7
  287.5 229.0 %all-to-all-start = ((bf16[64,3,32,128]{3,2,1,0:T(8,128)(2,1)}), bf16[64,3,32,128]{3,2,1,0:T(8,128)(2,1)}, u32[]{:S(2)}, u32[]{:S(2)}) async-start(bf16[64,3,32,128]{3,2,1,0:T(8,128)(2,1)} %stack.104), calls=%async_computation | async-start | bytes 3145728 | tf_op jit(solution)/shard_map/all_to_all | solution.py:179
  297.3 6.9 %copy-start.14 = (bf16[128,32,128]{2,1,0:T(8,128)(2,1)S(1)}, bf16[128,32,128]{2,1,0:T(8,128)(2,1)}, u32[]{:S(2)}) copy-start(bf16[128,32,128]{2,1,0:T(8,128)(2,1)} %param.13) | copy-start | bytes 3145732
  304.2 4.0 copy-start.6
  304.2 4.0 copy-start.8
  518.2 13.1 %copy-start.124 = (pred[32]{0:T(512)(128)(4,1)S(1)}, pred[32]{0:T(512)(128)(4,1)}, u32[]{:S(2)}) copy-start(pred[32]{0:T(512)(128)(4,1)} %compare_and_fusion) | copy-start | bytes 100
  518.2 14.2 %copy-start.23 = (bf16[128,32,128]{2,0,1:T(8,128)(2,1)S(1)}, bf16[128,32,128]{2,0,1:T(8,128)(2,1)}, u32[]{:S(2)}) copy-start(bf16[128,32,128]{2,0,1:T(8,128)(2,1)} %get-tuple-element.96) | copy-start | bytes 3145732
  518.2 14.2 %copy-start.41 = (f32[128,32]{0,1:T(8,128)S(1)}, f32[128,32]{0,1:T(8,128)}, u32[]{:S(2)}) copy-start(f32[128,32]{0,1:T(8,128)} %convert_element_type.492) | copy-start | bytes 49156
  (91 other events, 184.3 us)
Sparse Core Ops, SparseCore 0:
  16.0 109.2 all-gather.1
  250.6 260.4 all-reduce.3
